TPU v7x, 256 devices: a whole 4x4x8 slice. The times are simulated.
256 devices in a mesh: gx: 16 (over z_hi, y, core), gy: 16 (over x, z_lo).
Axes of the slice: x: 4, y: 4, z: 8 (z_hi: 2, z_lo: 4; z = z_hi * 4 + z_lo), core: 2. Of those that a mesh axis runs over, the one named last changes fastest.
Arguments:
- adjoint_rhs: float32 [32, 16, 768, 128], P('gx', 'gy'), may hold values from -6 to 6
- local_inverse: bfloat16 [32, 16, 1024, 768], P('gx', 'gy')
- local_operator: bfloat16 [32, 16, 1024, 768], P('gx', 'gy')
- spill_rows: int32 [32, 16, 4, 64], P('gx', 'gy'), may hold values from 0 to 767, as said below
- coarse_basis: bfloat16 [32, 16, 64, 768], P('gx', 'gy'), may hold values from -3 to 3
- coarse_ids: int32 [32, 16, 64], P('gx', 'gy'), may hold values from 0 to 1023
- coarse_inverse: bfloat16 [1024, 1024], P(('gx', 'gy')), may hold values from -0.00030517578 to 0.00030517578
Outputs:
- adjoint_solution: float32 [32, 16, 768, 128], P('gx', 'gy')
- residual: float32 [32, 16, 768, 128], P('gx', 'gy')
Inputs may be any that keep to these rules, and one draw needn't show every extreme that they name: Each list of spill_rows holds 64 distinct rows. `coarse_ids`: A coarse function may be listed more than once for a subdomain.
All inputs are finite; a program needn't handle non-finite values.
Results may differ from a plain program's by a relative error of at most 0.0041.
Values may be sent and summed in bfloat16 or wider, within the bound.
A program may use at most 64 MiB of HBM per device.

v0:
```python
import jax
import jax.numpy as jnp
from jax import lax
from jax.sharding import PartitionSpec as P


def with_halo(block, sides, width):
    for axis, dim in sides:
        count = lax.axis_size(axis)
        forward = [(i, i + 1) for i in range(count - 1)]
        backward = [(target, source) for source, target in forward]
        low = lax.ppermute(
            lax.slice_in_dim(block, block.shape[dim] - width, None, axis=dim), axis, forward
        )
        high = lax.ppermute(lax.slice_in_dim(block, 0, width, axis=dim), axis, backward)
        block = jnp.concatenate([low, block, high], axis=dim)
    return block


def add_rows(owned_rows, indices, values):
    return owned_rows.at[indices].add(values)


def spread(extended, indices):
    sub_count = extended.shape[0]
    group_rows = indices.shape[1] // 4
    owned_count = extended.shape[1] - 4 * group_rows
    owned_rows = extended[:, :owned_count]
    groups = extended[:, owned_count:].reshape(sub_count, 4, group_rows, extended.shape[2])
    outward = jnp.stack([groups[0, 0], groups[sub_count - 1, 1]])
    across = with_halo(outward, (("gx", 0),), 1)
    from_west = jnp.concatenate([across[0][None], groups[:-1, 1]], 0)
    from_east = jnp.concatenate([groups[1:, 0], across[3][None]], 0)
    vertical = jnp.stack([groups[:, 2], groups[:, 3]])
    beside = with_halo(vertical, (("gy", 0),), 1)
    received = jnp.stack([from_west, from_east, beside[0], beside[3]], 1).reshape(
        sub_count, 4 * group_rows, extended.shape[2]
    )
    return jax.vmap(add_rows)(owned_rows, indices, received)


def body(
    adjoint_rhs, local_inverse, local_operator, spill_rows, coarse_basis, coarse_ids, coarse_inverse
):
    highest = lax.Precision.HIGHEST
    contract_first = (((0,), (0,)), ((), ()))
    residual = adjoint_rhs[:, 0]
    inverses = local_inverse[:, 0]
    operators = local_operator[:, 0]
    indices = spill_rows[:, 0].reshape(spill_rows.shape[0], -1)
    basis_rows = coarse_basis[:, 0].astype(jnp.float32)
    sub_count = coarse_ids.shape[0]
    functions = coarse_ids.shape[2]
    coarse_order = coarse_inverse.shape[1]
    flat_ids = coarse_ids[:, 0].reshape(-1)
    one_hot = (flat_ids[None, :] == jnp.arange(coarse_order, dtype=jnp.int32)[:, None]).astype(
        jnp.float32
    )
    terms = jnp.einsum("skn,snr->skr", basis_rows, residual, precision=highest)
    local_sums = jnp.dot(
        one_hot, terms.reshape(sub_count * functions, terms.shape[2]), precision=highest
    )
    shares = lax.psum_scatter(local_sums, ("gx", "gy"), scatter_dimension=0, tiled=True)
    partial_sol = lax.dot_general(
        coarse_inverse,
        shares.astype(jnp.bfloat16),
        contract_first,
        preferred_element_type=jnp.float32,
    )
    coarse_sol = lax.psum(partial_sol, ("gx", "gy"))
    local_sol = jnp.einsum(
        "sln,snr->slr", inverses, residual.astype(jnp.bfloat16), preferred_element_type=jnp.float32
    )
    picked = jnp.dot(one_hot.T, coarse_sol, precision=highest).reshape(
        sub_count, functions, coarse_sol.shape[1]
    )
    coarse_part = jnp.einsum("skn,skr->snr", basis_rows, picked, precision=highest)
    correction = spread(local_sol, indices) + coarse_part
    image = jnp.einsum(
        "sln,snr->slr",
        operators,
        correction.astype(jnp.bfloat16),
        preferred_element_type=jnp.float32,
    )
    residual = residual - spread(image, indices)
    return (correction[:, None], residual[:, None])


def solution(mesh):
    in_specs = (
        P("gx", "gy", None, None),
        P("gx", "gy", None, None),
        P("gx", "gy", None, None),
        P("gx", "gy", None, None),
        P("gx", "gy", None, None),
        P("gx", "gy", None),
        P(("gx", "gy"), None),
    )
    out_specs = (P("gx", "gy", None, None), P("gx", "gy", None, None))
    return jax.shard_map(body, mesh=mesh, in_specs=in_specs, out_specs=out_specs, check_vma=False)
```

profile of v0, /device:TPU:226, one launch (start us, length us, event | category | flops | bytes accessed | tf_op | source)
XLA Modules:
  0.0 501.2 jit_solution(17594343954247628550)
XLA Ops:
  7.7 1.6 reduce.3
  9.5 1.6 fusion.8
  11.1 1.2 fusion.12
  12.3 75.3 %all-reduce.5 = bf16[1024,128]{1,0:T(8,128)(2,1)S(1)} all-reduce(f32[1024,128]{1,0:T(8,128)} %fusion.12), channel_id=2, replica_groups=mesh['gx'=16,'gy'=16] {'gx','gy'}, use_global_device_ids=true, to_apply=%region_0.0.clone | all-reduce | flops 131072 | bytes 786432
  87.6 1.8 convolution_bitcast_fusion.1
  89.4 2.1 fusion.2
  91.5 1.0 copy-done.1
  93.2 3.7 collective-permute-start
  96.8 7.9 %collective-permute-start.1 = (f32[1,64,128]{2,1,0:T(8,128)}, f32[1,64,128]{2,1,0:T(8,128)S(1)}, u32[]{:S(2)}, u32[]{:S(2)}) collective-permute-start(f32[1,64,128]{2,1,0:T(8,128)} %get-tuple-element.15), channel_id=1, source_target_pairs={{16,0},{32,16},{48,32},{64,48},{80,64},{96,80},{112,96},{128,112},... | collective-permute-start | bytes 98312 | tf_op jit(solution)/shard_map/ppermute | solution.py:15
  104.8 5.4 %collective-permute-start.2 = (f32[1,2,64,128]{3,2,1,0:T(8,128)S(1)}, f32[1,2,64,128]{3,2,1,0:T(8,128)S(1)}, u32[]{:S(2)}, u32[]{:S(2)}) collective-permute-start(f32[1,2,64,128]{3,2,1,0:T(8,128)S(1)} %get-tuple-element.18), channel_id=1, source_target_pairs={{0,1},{1,2},{2,3},{3,4},{4,5},{5,6},{6,7},{7,8},{8,9},{9,10},{10,1... | collective-permute-start | bytes 196616 | tf_op jit(solution)/shard_map/ppermute | solution.py:12
  110.1 1.9 collective-permute-start.3
  112.2 6.8 %collective-permute-done.3 = f32[1,2,64,128]{3,2,1,0:T(8,128)S(1)} collective-permute-done((f32[1,2,64,128]{3,2,1,0:T(8,128)S(1)}, f32[1,2,64,128]{3,2,1,0:T(8,128)S(1)}, u32[]{:S(2)}, u32[]{:S(2)}) %collective-permute-start.3) | collective-permute-done | bytes 65568 | tf_op jit(solution)/shard_map/ppermute | solution.py:15
  119.1 224.2 %all-reduce.4.cloned.1.call-done = f32[1024,128]{0,1:T(8,128)} async-done(((f32[1024,128]{0,1:T(8,128)}), f32[1024,128]{0,1:T(8,128)}) %all-reduce.4.cloned.1.call-update) | async-done | bytes 524304 | tf_op jit(solution)/shard_map/psum | solution.py:70
  343.3 1.5 fusion.14
  344.9 2.7 fusion.7
  347.5 54.2 %scatter_fusion = f32[2,768,128]{2,1,0:T(8,128)} fusion(f32[2,768,128]{2,1,0:T(8,128)} %fusion.7, s32[512]{0:T(512)S(1)} %bitcast.99, f32[512,128]{1,0:T(8,128)S(1)} %bitcast.102), kind=kCustom, calls=%fused_computation | custom fusion | flops 65536 | bytes 790528 | tf_op jit(solution)/shard_map/vmap()/scatter-add | solution.py:21
  401.7 3.3 fusion.4
  405.0 1.0 copy-done.2
  406.0 0.7 slice.77
  406.7 1.1 copy.38
  407.8 0.6 slice_bitcast_fusion.7
  408.5 3.2 collective-permute-start.4
  411.7 0.6 slice_bitcast_fusion.1
  412.3 2.1 slice.76
  414.4 2.3 copy.41
  416.7 8.3 %collective-permute-start.5 = (f32[1,64,128]{2,1,0:T(8,128)S(1)}, f32[1,64,128]{2,1,0:T(8,128)S(1)}, u32[]{:S(2)}, u32[]{:S(2)}) collective-permute-start(f32[1,64,128]{2,1,0:T(8,128)S(1)} %copy-done.4), channel_id=1, source_target_pairs={{16,0},{32,16},{48,32},{64,48},{80,64},{96,80},{112,96},{128,112},... | collective-permute-start | bytes 98312 | tf_op jit(solution)/shard_map/ppermute | solution.py:15
  425.1 6.7 %collective-permute-start.6 = (f32[1,2,64,128]{3,2,1,0:T(8,128)S(1)}, f32[1,2,64,128]{3,2,1,0:T(8,128)S(1)}, u32[]{:S(2)}, u32[]{:S(2)}) collective-permute-start(f32[1,2,64,128]{3,2,1,0:T(8,128)S(1)} %copy-done.3), channel_id=1, source_target_pairs={{0,1},{1,2},{2,3},{3,4},{4,5},{5,6},{6,7},{7,8},{8,9},{9,10},{10,1... | collective-permute-start | bytes 196616 | tf_op jit(solution)/shard_map/ppermute | solution.py:12
  431.8 1.9 collective-permute-start.7
  433.8 0.8 maximum_bitcast_fusion.2
  434.5 6.1 %collective-permute-done.7 = f32[1,2,64,128]{3,2,1,0:T(8,128)S(1)} collective-permute-done((f32[1,2,64,128]{3,2,1,0:T(8,128)S(1)}, f32[1,2,64,128]{3,2,1,0:T(8,128)S(1)}, u32[]{:S(2)}, u32[]{:S(2)}) %collective-permute-start.7) | collective-permute-done | bytes 65568 | tf_op jit(solution)/shard_map/ppermute | solution.py:15
  440.7 51.3 %scatter_fusion.1 = f32[2,768,128]{2,1,0:T(8,128)} fusion(f32[2,768,128]{2,1,0:T(8,128)} %copy.41, s32[512]{0:T(512)S(1)} %bitcast.100, f32[512,128]{1,0:T(8,128)S(1)} %bitcast.103), kind=kCustom, calls=%fused_computation.1 | custom fusion | flops 65536 | bytes 790528 | tf_op jit(solution)/shard_map/vmap()/scatter-add | solution.py:21
  492.0 2.3 fusion.10
  (33 shorter events, 1.5 us)
Async XLA Ops:
  7.2 82.2 %copy-start = (bf16[2,1,1024,768]{3,2,1,0:T(8,128)(2,1)S(1)}, bf16[2,1,1024,768]{3,2,1,0:T(8,128)(2,1)}, u32[]{:S(2)}) copy-start(bf16[2,1,1024,768]{3,2,1,0:T(8,128)(2,1)} %param.8) | copy-start | bytes 9437188
  7.2 336.2 %all-reduce.4.cloned.1.call-start = ((), (), s32[]{:S(2)}) async-start(), calls=%async_computation | async-start | bytes 1048576 | tf_op jit(solution)/shard_map/psum | solution.py:70
  89.4 22.7 %copy-start.5 = (s32[2,1,4,64]{3,2,1,0:T(4,128)S(1)}, s32[2,1,4,64]{3,2,1,0:T(4,128)}, u32[]{:S(2)}) copy-start(s32[2,1,4,64]{3,2,1,0:T(4,128)} %param.10) | copy-start | bytes 6148
  91.5 1.0 copy-start.1
  93.2 19.0 %collective-permute-start = (f32[1,64,128]{2,1,0:T(8,128)}, f32[1,64,128]{2,1,0:T(8,128)S(1)}, u32[]{:S(2)}, u32[]{:S(2)}) collective-permute-start(f32[1,64,128]{2,1,0:T(8,128)} %get-tuple-element.14), channel_id=1, source_target_pairs={{0,16},{16,32},{32,48},{48,64},{64,80},{80,96},{96,112},{112,128},... | collective-permute-start | bytes 98312 | tf_op jit(solution)/shard_map/ppermute | solution.py:12
  96.8 15.4 %collective-permute-start.1 = (f32[1,64,128]{2,1,0:T(8,128)}, f32[1,64,128]{2,1,0:T(8,128)S(1)}, u32[]{:S(2)}, u32[]{:S(2)}) collective-permute-start(f32[1,64,128]{2,1,0:T(8,128)} %get-tuple-element.15), channel_id=1, source_target_pairs={{16,0},{32,16},{48,32},{64,48},{80,64},{96,80},{112,96},{128,112},... | collective-permute-start | bytes 98312 | tf_op jit(solution)/shard_map/ppermute | solution.py:15
  104.8 7.5 %collective-permute-start.2 = (f32[1,2,64,128]{3,2,1,0:T(8,128)S(1)}, f32[1,2,64,128]{3,2,1,0:T(8,128)S(1)}, u32[]{:S(2)}, u32[]{:S(2)}) collective-permute-start(f32[1,2,64,128]{3,2,1,0:T(8,128)S(1)} %get-tuple-element.18), channel_id=1, source_target_pairs={{0,1},{1,2},{2,3},{3,4},{4,5},{5,6},{6,7},{7,8},{8,9},{9,10},{10,1... | collective-permute-start | bytes 196616 | tf_op jit(solution)/shard_map/ppermute | solution.py:12
  110.1 8.9 %collective-permute-start.3 = (f32[1,2,64,128]{3,2,1,0:T(8,128)S(1)}, f32[1,2,64,128]{3,2,1,0:T(8,128)S(1)}, u32[]{:S(2)}, u32[]{:S(2)}) collective-permute-start(f32[1,2,64,128]{3,2,1,0:T(8,128)S(1)} %get-tuple-element.19), channel_id=1, source_target_pairs={{1,0},{2,1},{3,2},{4,3},{5,4},{6,5},{7,6},{8,7},{9,8},{10,9},{11,1... | collective-permute-start | bytes 196616 | tf_op jit(solution)/shard_map/ppermute | solution.py:15
  405.0 1.0 copy-start.2
  408.5 25.3 %collective-permute-start.4 = (f32[1,64,128]{2,1,0:T(8,128)}, f32[1,64,128]{2,1,0:T(8,128)}, u32[]{:S(2)}, u32[]{:S(2)}) collective-permute-start(f32[1,64,128]{2,1,0:T(8,128)} %get-tuple-element.8), channel_id=1, source_target_pairs={{0,16},{16,32},{32,48},{48,64},{64,80},{80,96},{96,112},{112,128},... | collective-permute-start | bytes 98312 | tf_op jit(solution)/shard_map/ppermute | solution.py:12
  412.3 4.4 copy-start.4
  412.3 12.8 %copy-start.3 = (f32[1,2,64,128]{3,2,1,0:T(8,128)S(1)}, f32[1,2,64,128]{3,2,1,0:T(8,128)}, u32[]{:S(2)}) copy-start(f32[1,2,64,128]{3,2,1,0:T(8,128)} %get-tuple-element.12) | copy-start | bytes 196612
  416.7 17.8 %collective-permute-start.5 = (f32[1,64,128]{2,1,0:T(8,128)S(1)}, f32[1,64,128]{2,1,0:T(8,128)S(1)}, u32[]{:S(2)}, u32[]{:S(2)}) collective-permute-start(f32[1,64,128]{2,1,0:T(8,128)S(1)} %copy-done.4), channel_id=1, source_target_pairs={{16,0},{32,16},{48,32},{64,48},{80,64},{96,80},{112,96},{128,112},... | collective-permute-start | bytes 98312 | tf_op jit(solution)/shard_map/ppermute | solution.py:15
  425.1 9.5 %collective-permute-start.6 = (f32[1,2,64,128]{3,2,1,0:T(8,128)S(1)}, f32[1,2,64,128]{3,2,1,0:T(8,128)S(1)}, u32[]{:S(2)}, u32[]{:S(2)}) collective-permute-start(f32[1,2,64,128]{3,2,1,0:T(8,128)S(1)} %copy-done.3), channel_id=1, source_target_pairs={{0,1},{1,2},{2,3},{3,4},{4,5},{5,6},{6,7},{7,8},{8,9},{9,10},{10,1... | collective-permute-start | bytes 196616 | tf_op jit(solution)/shard_map/ppermute | solution.py:12
  431.8 8.9 %collective-permute-start.7 = (f32[1,2,64,128]{3,2,1,0:T(8,128)S(1)}, f32[1,2,64,128]{3,2,1,0:T(8,128)S(1)}, u32[]{:S(2)}, u32[]{:S(2)}) collective-permute-start(f32[1,2,64,128]{3,2,1,0:T(8,128)S(1)} %get-tuple-element.13), channel_id=1, source_target_pairs={{1,0},{2,1},{3,2},{4,3},{5,4},{6,5},{7,6},{8,7},{9,8},{10,9},{11,1... | collective-permute-start | bytes 196616 | tf_op jit(solution)/shard_map/ppermute | solution.py:15
Sparse Core Ops, SparseCore 0:
  89.5 253.7 all-reduce.3
where the time goes:
time: 504 us; the launch traced here: 501 us
  waiting for transfers between devices  237 us (47%)
  other arithmetic  110 us (22%)
  blocking collectives  75.3 us (15%)
  starting transfers between devices  39.1 us (8%)
  between operations  14.3 us (3%)
  matrix products  14.2 us (3%)
  local copies, waits for them, and re-layouts  10.8 us (2%)
    psum x1, waiting for transfers between devices, body(): coarse_sol = lax.psum(partial_sol, ('gx', 'gy'))  224 us
    scatter-add x2, other arithmetic, add_rows(): return owned_rows.at[indices].add(values)  105 us
    unnamed x1, blocking collectives  75.3 us
    ppermute x4, starting transfers between devices, with_halo(): lax.ppermute(lax.slice_in_dim(block, 0, width, axis=dim), axis, backward)  20.1 us
    ppermute x4, starting transfers between devices, with_halo(): lax.ppermute(lax.slice_in_dim(block, block.shape[dim] - width, None, axis...  19 us
    ppermute x4, waiting for transfers between devices, with_halo(): lax.ppermute(lax.slice_in_dim(block, 0, width, axis=dim), axis, backward)  12.9 us
  transfers between devices with their start and end apart: 9, of which 3 were waited for; matrix products, arithmetic and copies ran while one was open for 2% of the time, Pallas kernels for 0%

commit v1 on v0

--- a/solution.py
+++ b/solution.py
@@ -67,7 +67,8 @@
         contract_first,
         preferred_element_type=jnp.float32,
     )
-    coarse_sol = lax.psum(partial_sol, ("gx", "gy"))
+    one_axis = lax.psum(partial_sol, "gy")
+    coarse_sol = lax.psum(one_axis, "gx")
     local_sol = jnp.einsum(
         "sln,snr->slr", inverses, residual.astype(jnp.bfloat16), preferred_element_type=jnp.float32
     )

time: 504 us -> 592 us (1.17)
  waiting for transfers between devices: 237 us -> 326 us
    psum x1 -> x2, waiting for transfers between devices: 224 us -> 320 us  [the longest x1 188 us: body(): coarse_sol = lax.psum(one_axis, 'gx')]
    ppermute x4, waiting for transfers between devices: 12.9 us -> 6.14 us  [with_halo(): lax.ppermute(lax.slice_in_dim(block, 0, width, axis=dim), axis, backward)]
  transfers between devices with their start and end apart: 9 -> 10, of which waited for: 3 -> 3; matrix products, arithmetic and copies ran while one was open for 2% -> 1% of each run, Pallas kernels for 0% -> 0%
where the time goes in v1:
time: 592 us; the launch traced here: 589 us
  waiting for transfers between devices  326 us (55%)
  other arithmetic  110 us (19%)
  blocking collectives  75.3 us (13%)
  starting transfers between devices  38.2 us (6%)
  between operations  14.3 us (2%)
  matrix products  14.2 us (2%)
  local copies, waits for them, and re-layouts  10.8 us (2%)
    psum x1, waiting for transfers between devices, body(): coarse_sol = lax.psum(one_axis, 'gx')  188 us
    psum x1, waiting for transfers between devices, body(): one_axis = lax.psum(partial_sol, 'gy')  132 us
    scatter-add x2, other arithmetic, add_rows(): return owned_rows.at[indices].add(values)  105 us
    unnamed x1, blocking collectives  75.3 us
    ppermute x4, starting transfers between devices, with_halo(): lax.ppermute(lax.slice_in_dim(block, 0, width, axis=dim), axis, backward)  21.4 us
    ppermute x4, starting transfers between devices, with_halo(): lax.ppermute(lax.slice_in_dim(block, block.shape[dim] - width, None, axis...  16.8 us
  transfers between devices with their start and end apart: 10, of which 3 were waited for; matrix products, arithmetic and copies ran while one was open for 1% of the time, Pallas kernels for 0%

profile of v1, /device:TPU:226, one launch (start us, length us, event | category | flops | bytes accessed | tf_op | source)
XLA Modules:
  0.0 589.1 jit_solution(353823025265678290)
XLA Ops:
  7.7 1.6 reduce.3
  9.5 1.6 fusion.8
  11.1 1.2 fusion.12
  12.3 75.3 %all-reduce.8 = bf16[1024,128]{1,0:T(8,128)(2,1)S(1)} all-reduce(f32[1024,128]{1,0:T(8,128)} %fusion.12), channel_id=2, replica_groups=mesh['gx'=16,'gy'=16] {'gx','gy'}, use_global_device_ids=true, to_apply=%region_0.0.clone | all-reduce | flops 131072 | bytes 786432
  87.6 1.8 convolution_bitcast_fusion.1
  89.5 2.1 fusion.2
  91.6 1.0 copy-done.1
  92.6 0.6 slice_bitcast_fusion.11
  93.2 3.7 collective-permute-start
  96.9 7.9 %collective-permute-start.1 = (f32[1,64,128]{2,1,0:T(8,128)}, f32[1,64,128]{2,1,0:T(8,128)S(1)}, u32[]{:S(2)}, u32[]{:S(2)}) collective-permute-start(f32[1,64,128]{2,1,0:T(8,128)} %get-tuple-element.15), channel_id=1, source_target_pairs={{16,0},{32,16},{48,32},{64,48},{80,64},{96,80},{112,96},{128,112},... | collective-permute-start | bytes 98312 | tf_op jit(solution)/shard_map/ppermute | solution.py:15
  104.8 5.4 collective-permute-start.2
  110.2 1.9 collective-permute-start.3
  112.2 132.2 %all-reduce.5.cloned.1.call-done = f32[1024,128]{0,1:T(8,128)} async-done(((f32[1024,128]{0,1:T(8,128)}), f32[1024,128]{0,1:T(8,128)}) %all-reduce.5.cloned.1.call-update) | async-done | bytes 524304 | tf_op jit(solution)/shard_map/psum | solution.py:70
  244.6 187.6 %all-reduce.7.cloned.1.call-done = f32[1024,128]{0,1:T(8,128)} async-done(((f32[1024,128]{0,1:T(8,128)}), f32[1024,128]{0,1:T(8,128)}) %all-reduce.7.cloned.1.call-update) | async-done | bytes 524304 | tf_op jit(solution)/shard_map/psum | solution.py:71
  432.2 1.5 fusion.14
  433.7 2.7 fusion.7
  436.4 54.2 %scatter_fusion = f32[2,768,128]{2,1,0:T(8,128)} fusion(f32[2,768,128]{2,1,0:T(8,128)} %fusion.7, s32[512]{0:T(512)S(1)} %bitcast.99, f32[512,128]{1,0:T(8,128)S(1)} %bitcast.102), kind=kCustom, calls=%fused_computation | custom fusion | flops 65536 | bytes 790528 | tf_op jit(solution)/shard_map/vmap()/scatter-add | solution.py:21
  490.6 3.3 fusion.4
  493.9 1.0 copy-done.2
  494.9 0.7 slice.77
  495.6 1.1 copy.38
  496.7 0.6 slice_bitcast_fusion.7
  497.3 1.9 collective-permute-start.4
  499.9 2.1 slice.76
  502.0 2.3 copy.41
  504.3 9.6 %collective-permute-start.5 = (f32[1,64,128]{2,1,0:T(8,128)S(1)}, f32[1,64,128]{2,1,0:T(8,128)S(1)}, u32[]{:S(2)}, u32[]{:S(2)}) collective-permute-start(f32[1,64,128]{2,1,0:T(8,128)S(1)} %copy-done.4), channel_id=1, source_target_pairs={{16,0},{32,16},{48,32},{64,48},{80,64},{96,80},{112,96},{128,112},... | collective-permute-start | bytes 98312 | tf_op jit(solution)/shard_map/ppermute | solution.py:15
  513.9 5.8 collective-permute-start.6
  519.7 1.9 collective-permute-start.7
  521.7 0.8 maximum_bitcast_fusion.2
  522.5 6.1 %collective-permute-done.7 = f32[1,2,64,128]{3,2,1,0:T(8,128)S(1)} collective-permute-done((f32[1,2,64,128]{3,2,1,0:T(8,128)S(1)}, f32[1,2,64,128]{3,2,1,0:T(8,128)S(1)}, u32[]{:S(2)}, u32[]{:S(2)}) %collective-permute-start.7) | collective-permute-done | bytes 65568 | tf_op jit(solution)/shard_map/ppermute | solution.py:15
  528.7 51.3 %scatter_fusion.1 = f32[2,768,128]{2,1,0:T(8,128)} fusion(f32[2,768,128]{2,1,0:T(8,128)} %copy.41, s32[512]{0:T(512)S(1)} %bitcast.100, f32[512,128]{1,0:T(8,128)S(1)} %bitcast.103), kind=kCustom, calls=%fused_computation.1 | custom fusion | flops 65536 | bytes 790528 | tf_op jit(solution)/shard_map/vmap()/scatter-add | solution.py:21
  579.9 2.3 fusion.10
  (36 shorter events, 1.6 us)
Async XLA Ops:
  7.2 82.3 %copy-start = (bf16[2,1,1024,768]{3,2,1,0:T(8,128)(2,1)S(1)}, bf16[2,1,1024,768]{3,2,1,0:T(8,128)(2,1)}, u32[]{:S(2)}) copy-start(bf16[2,1,1024,768]{3,2,1,0:T(8,128)(2,1)} %param.8) | copy-start | bytes 9437188
  7.2 237.2 %all-reduce.5.cloned.1.call-start = ((), (), s32[]{:S(2)}) async-start(), calls=%async_computation | async-start | bytes 1048576 | tf_op jit(solution)/shard_map/psum | solution.py:70
  89.4 22.7 %copy-start.5 = (s32[2,1,4,64]{3,2,1,0:T(4,128)S(1)}, s32[2,1,4,64]{3,2,1,0:T(4,128)}, u32[]{:S(2)}) copy-start(s32[2,1,4,64]{3,2,1,0:T(4,128)} %param.10) | copy-start | bytes 6148
  89.4 342.8 %all-reduce.7.cloned.1.call-start = ((), (), s32[]{:S(2)}) async-start(), calls=%async_computation.1 | async-start | bytes 1048576 | tf_op jit(solution)/shard_map/psum | solution.py:71
  91.6 1.0 copy-start.1
  93.2 151.3 %collective-permute-start = (f32[1,64,128]{2,1,0:T(8,128)}, f32[1,64,128]{2,1,0:T(8,128)S(1)}, u32[]{:S(2)}, u32[]{:S(2)}) collective-permute-start(f32[1,64,128]{2,1,0:T(8,128)} %get-tuple-element.14), channel_id=1, source_target_pairs={{0,16},{16,32},{32,48},{48,64},{64,80},{80,96},{96,112},{112,128},... | collective-permute-start | bytes 98312 | tf_op jit(solution)/shard_map/ppermute | solution.py:12
  96.9 147.6 %collective-permute-start.1 = (f32[1,64,128]{2,1,0:T(8,128)}, f32[1,64,128]{2,1,0:T(8,128)S(1)}, u32[]{:S(2)}, u32[]{:S(2)}) collective-permute-start(f32[1,64,128]{2,1,0:T(8,128)} %get-tuple-element.15), channel_id=1, source_target_pairs={{16,0},{32,16},{48,32},{64,48},{80,64},{96,80},{112,96},{128,112},... | collective-permute-start | bytes 98312 | tf_op jit(solution)/shard_map/ppermute | solution.py:15
  104.8 139.7 %collective-permute-start.2 = (f32[1,2,64,128]{3,2,1,0:T(8,128)S(1)}, f32[1,2,64,128]{3,2,1,0:T(8,128)S(1)}, u32[]{:S(2)}, u32[]{:S(2)}) collective-permute-start(f32[1,2,64,128]{3,2,1,0:T(8,128)S(1)} %get-tuple-element.18), channel_id=1, source_target_pairs={{0,1},{1,2},{2,3},{3,4},{4,5},{5,6},{6,7},{7,8},{8,9},{9,10},{10,1... | collective-permute-start | bytes 196616 | tf_op jit(solution)/shard_map/ppermute | solution.py:12
  110.2 134.3 %collective-permute-start.3 = (f32[1,2,64,128]{3,2,1,0:T(8,128)S(1)}, f32[1,2,64,128]{3,2,1,0:T(8,128)S(1)}, u32[]{:S(2)}, u32[]{:S(2)}) collective-permute-start(f32[1,2,64,128]{3,2,1,0:T(8,128)S(1)} %get-tuple-element.19), channel_id=1, source_target_pairs={{1,0},{2,1},{3,2},{4,3},{5,4},{6,5},{7,6},{8,7},{9,8},{10,9},{11,1... | collective-permute-start | bytes 196616 | tf_op jit(solution)/shard_map/ppermute | solution.py:15
  493.9 1.0 copy-start.2
  497.3 24.4 %collective-permute-start.4 = (f32[1,64,128]{2,1,0:T(8,128)}, f32[1,64,128]{2,1,0:T(8,128)}, u32[]{:S(2)}, u32[]{:S(2)}) collective-permute-start(f32[1,64,128]{2,1,0:T(8,128)} %get-tuple-element.8), channel_id=1, source_target_pairs={{0,16},{16,32},{32,48},{48,64},{64,80},{80,96},{96,112},{112,128},... | collective-permute-start | bytes 98312 | tf_op jit(solution)/shard_map/ppermute | solution.py:12
  499.9 4.4 copy-start.4
  499.9 14.1 %copy-start.3 = (f32[1,2,64,128]{3,2,1,0:T(8,128)S(1)}, f32[1,2,64,128]{3,2,1,0:T(8,128)}, u32[]{:S(2)}) copy-start(f32[1,2,64,128]{3,2,1,0:T(8,128)} %get-tuple-element.12) | copy-start | bytes 196612
  504.3 18.2 %collective-permute-start.5 = (f32[1,64,128]{2,1,0:T(8,128)S(1)}, f32[1,64,128]{2,1,0:T(8,128)S(1)}, u32[]{:S(2)}, u32[]{:S(2)}) collective-permute-start(f32[1,64,128]{2,1,0:T(8,128)S(1)} %copy-done.4), channel_id=1, source_target_pairs={{16,0},{32,16},{48,32},{64,48},{80,64},{96,80},{112,96},{128,112},... | collective-permute-start | bytes 98312 | tf_op jit(solution)/shard_map/ppermute | solution.py:15
  513.9 8.5 %collective-permute-start.6 = (f32[1,2,64,128]{3,2,1,0:T(8,128)S(1)}, f32[1,2,64,128]{3,2,1,0:T(8,128)S(1)}, u32[]{:S(2)}, u32[]{:S(2)}) collective-permute-start(f32[1,2,64,128]{3,2,1,0:T(8,128)S(1)} %copy-done.3), channel_id=1, source_target_pairs={{0,1},{1,2},{2,3},{3,4},{4,5},{5,6},{6,7},{7,8},{8,9},{9,10},{10,1... | collective-permute-start | bytes 196616 | tf_op jit(solution)/shard_map/ppermute | solution.py:12
  519.7 8.9 %collective-permute-start.7 = (f32[1,2,64,128]{3,2,1,0:T(8,128)S(1)}, f32[1,2,64,128]{3,2,1,0:T(8,128)S(1)}, u32[]{:S(2)}, u32[]{:S(2)}) collective-permute-start(f32[1,2,64,128]{3,2,1,0:T(8,128)S(1)} %get-tuple-element.13), channel_id=1, source_target_pairs={{1,0},{2,1},{3,2},{4,3},{5,4},{6,5},{7,6},{8,7},{9,8},{10,9},{11,1... | collective-permute-start | bytes 196616 | tf_op jit(solution)/shard_map/ppermute | solution.py:15
Sparse Core Ops, SparseCore 0:
  89.5 154.8 all-reduce.4
  247.0 185.1 all-reduce.6
